TPU v7x, 512 devices: a whole 4x8x8 slice. The times are simulated.
512 devices in a mesh: seg: 4 (over y_hi, core), pan: 128 (over y_lo, z, x).
Axes of the slice: x: 4, y: 8 (y_hi: 2, y_lo: 4; y = y_hi * 4 + y_lo), z: 8, core: 2. Of those that a mesh axis runs over, the one named last changes fastest.
Arguments:
- sources: bfloat16 [2, 2, 64, 1048576], P(None, None, 'seg', 'pan'), may hold values from -0.75 to 0.75
- panel_geom: float32 [6, 1048576], P(None, 'pan'), may hold values from -1 to 1, as said below
- mic_pos: float32 [3, 1024], replicated, may hold values from -12 to 12, as said below
- mic_order: int32 [1024], replicated, may hold values from 0 to 1023, each once
Outputs:
- csm: float32 [2, 1024, 1024], P(None, 'pan', 'seg')
Inputs may be any that keep to these rules, and one draw needn't show every extreme that they name: `mic_order`: each of the 1024 microphones stands exactly once. `panel_geom`: panel centres lie on a cylinder of radius 1 around the first axis with first coordinate within -1 to 1; normals are the unit radial directions. `mic_pos`: microphones lie at distances 6 to 12 from the anchor (0, 0, 0).
All inputs are finite; a program needn't handle non-finite values.
Results may differ from a plain program's by a relative error of at most 0.0039.
Values may be sent and summed in bfloat16 or wider, within the bound.
No kernel may reach another device: no remote copies, remote signals or barrier semaphores. Data moves between devices by JAX's collectives and lax.ppermute only.
A program may use at most 64 MiB of HBM per device.

v0:
```python
import math
import jax
import jax.numpy as jnp
from jax import lax
from jax.sharding import PartitionSpec as P

mach_number = 0.3
beta_sq = 0.91
wave_number = 40.0


def kernel_block(mics, geometry):
    dx = mics[0][:, None] - geometry[0][None, :]
    dy = mics[1][:, None] - geometry[1][None, :]
    dz = mics[2][:, None] - geometry[2][None, :]
    rstar = jnp.sqrt(dx * dx + beta_sq * (dy * dy + dz * dz))
    radius = (rstar - mach_number * dx) / beta_sq
    phase = wave_number * radius
    amplitude = 1.0 / (4.0 * math.pi * rstar)
    green_re = amplitude * jnp.cos(phase)
    green_im = -amplitude * jnp.sin(phase)
    normal_part = (
        dx * geometry[3][None, :] + dy * geometry[4][None, :] + dz * geometry[5][None, :]
    ) / rstar
    scale_re = normal_part / (wave_number * rstar)
    dip_re = scale_re * green_re - normal_part * green_im
    dip_im = scale_re * green_im + normal_part * green_re
    return jnp.concatenate([green_re, green_im, dip_re, dip_im], axis=1).astype(jnp.bfloat16)


def block_weights(piece):
    swapped = jnp.transpose(piece, (0, 1, 3, 2))
    real_cols = jnp.concatenate(
        [swapped[0, 0], -swapped[1, 0], swapped[0, 1], -swapped[1, 1]], axis=0
    )
    imag_cols = jnp.concatenate(
        [swapped[1, 0], swapped[0, 0], swapped[1, 1], swapped[0, 1]], axis=0
    )
    return jnp.concatenate([real_cols, imag_cols], axis=1)


def split_sources(sources, blocks, block_size):
    shaped = sources.reshape(2, 2, sources.shape[2], blocks, block_size)
    return jnp.transpose(shaped, (3, 0, 1, 2, 4))


def panel_spectra(mics, geom_blocks, source_blocks):

    def step(running, pair):
        geometry, piece = pair
        weights = block_weights(piece)
        return (
            running
            + jnp.dot(kernel_block(mics, geometry), weights, preferred_element_type=jnp.float32),
            None,
        )

    init = jnp.zeros((mics.shape[1], 2 * source_blocks.shape[3]), jnp.float32)
    summed, unused = lax.scan(step, init, (geom_blocks, source_blocks))
    return summed


def summed_spectra(mic_rows, geom_blocks, source_blocks):
    local_terms = panel_spectra(mic_rows, geom_blocks, source_blocks)
    return lax.psum(local_terms, "pan")


def cross_terms(own_rows, columns):
    half = columns.shape[1] // 2
    rows_re = own_rows[:, :half]
    rows_im = own_rows[:, half:]
    cols_re = columns[:, :half]
    cols_im = columns[:, half:]
    highest = lax.Precision.HIGHEST
    csm_re = jnp.dot(rows_re, cols_re.T, precision=highest) + jnp.dot(
        rows_im, cols_im.T, precision=highest
    )
    csm_im = jnp.dot(rows_im, cols_re.T, precision=highest) - jnp.dot(
        rows_re, cols_im.T, precision=highest
    )
    return jnp.stack([csm_re, csm_im])


def shards(sources, panel_geom, mic_pos, mic_order):
    ordered = jnp.take(mic_pos, mic_order, axis=1)
    panels_here = panel_geom.shape[1]
    block_size = min(512, panels_here)
    blocks = panels_here // block_size
    geom_blocks = jnp.transpose(panel_geom.reshape(6, blocks, block_size), (1, 0, 2))
    mics_all = ordered.shape[1]
    seg_count = lax.axis_size("seg")
    row_count = mics_all // lax.axis_size("pan")
    row_start = lax.axis_index("pan") * row_count
    source_blocks = split_sources(sources, blocks, block_size)
    spectra = summed_spectra(ordered, geom_blocks, source_blocks)
    own_rows = lax.dynamic_slice_in_dim(spectra, row_start, row_count, 0)
    partial_csm = cross_terms(own_rows, spectra)
    summed = lax.psum_scatter(partial_csm, "seg", scatter_dimension=2, tiled=True)
    return summed / (own_rows.shape[1] // 2 * seg_count)


def solution(mesh):
    placed = (P(None, None, "seg", "pan"), P(None, "pan"), P(), P())
    return jax.shard_map(
        shards, mesh=mesh, in_specs=placed, out_specs=P(None, "pan", "seg"), check_vma=False
    )
```

profile of v0, /device:TPU:1, one launch (start us, length us, event | category | flops | bytes accessed | tf_op | source)
XLA Modules:
  0.0 1561.1 jit_solution(7481023906343510673)
XLA Ops:
  9.0 2.8 gather_fusion
  14.1 267.6 %while.13 = (s32[]{:T(128)}, f32[1024,32]{0,1:T(8,128)S(1)}, f32[3,1024]{1,0:T(4,128)S(1)}, f32[16,6,512]{2,1,0:T(8,128)}, bf16[16,2,2,16,512]{4,3,2,1,0:T(8,128...) while((s32[]{:T(128)}, f32[1024,32]{0,1:T(8,128)S(1)}, ...), condition=%wide.region_1.2_spmd.clone, body=%wide.region_0.1_spmd.clone.sunk | while | flops 170999808 | bytes 9150687 | solution.py:59
  15.1 12.3 subtract_convert_fusion.2
  31.8 12.3 subtract_convert_fusion.2
  48.5 12.3 subtract_convert_fusion.2
  65.2 12.3 subtract_convert_fusion.2
  78.4 2.6 fusion.66
  81.9 12.3 subtract_convert_fusion.2
  98.7 12.3 subtract_convert_fusion.2
  111.8 2.6 fusion.66
  115.4 12.3 subtract_convert_fusion.2
  132.1 12.3 subtract_convert_fusion.2
  145.3 2.6 fusion.66
  148.8 12.3 subtract_convert_fusion.2
  162.0 2.6 fusion.66
  165.6 12.3 subtract_convert_fusion.2
  182.3 12.3 subtract_convert_fusion.2
  199.0 12.3 subtract_convert_fusion.2
  215.7 12.3 subtract_convert_fusion.2
  232.5 12.3 subtract_convert_fusion.2
  249.2 12.3 subtract_convert_fusion.2
  265.9 12.3 subtract_convert_fusion.2
  282.4 1203.3 %all-reduce.2.cloned.1.call-done = f32[1024,32]{0,1:T(8,128)} async-done(((f32[1024,32]{0,1:T(8,128)}), f32[1024,32]{0,1:T(8,128)}) %all-reduce.2.cloned.1.call-update) | async-done | bytes 131088 | tf_op jit(solution)/shard_map/psum | solution.py:65
  1491.1 61.8 %reduce-scatter.2.cloned.1.call-done = f32[2,8,256]{2,1,0:T(8,128)} async-done(((f32[2,8,1024]{2,1,0:T(8,128)}), f32[2,8,256]{2,1,0:T(8,128)}) %reduce-scatter.2.cloned.1.call-update) | async-done | bytes 16400 | tf_op jit(solution)/shard_map/reduce_scatter | solution.py:98
  (114 shorter events, 72.2 us)
Async XLA Ops:
  6.5 1479.1 %all-reduce.2.cloned.1.call-start = ((), (), s32[]{:S(2)}) async-start(), calls=%async_computation.1 | async-start | bytes 262144 | tf_op jit(solution)/shard_map/psum | solution.py:65
  7.9 4.2 copy-start
  281.6 0.7 copy-start.1
  282.3 1270.6 %reduce-scatter.2.cloned.1.call-start = ((), (), s32[]{:S(2)}) async-start(), calls=%async_computation.2 | async-start | bytes 81920 | tf_op jit(solution)/shard_map/reduce_scatter | solution.py:98
Sparse Core Ops, SparseCore 0:
  282.4 1203.1 all-reduce.1
  1491.2 61.6 reduce-scatter.1
where the time goes:
time: 1560 us
  waiting for transfers between devices  1270 us (81%)
  other arithmetic  200 us (13%)
  matrix products  45.8 us (3%)
  local copies, waits for them, and re-layouts  35.8 us (2%)
    psum x1, waiting for transfers between devices, summed_spectra(): return lax.psum(local_terms, 'pan')  1200 us
    another operation x16, other arithmetic  196 us
    reduce_scatter x1, waiting for transfers between devices, shards(): lax.psum_scatter(partial_csm, 'seg', scatter_dimension=2, tiled=True)  61.8 us
    dot_general x16, matrix products, step(): jnp.dot(kernel_block(mics, geometry), weights, preferred_element_type=jnp...  41.1 us
  transfers between devices with their start and end apart: 2, of which 2 were waited for; matrix products, arithmetic and copies ran while one was open for 0% of the time, Pallas kernels for 0%

commit v1 on v0

--- a/solution.py
+++ b/solution.py
@@ -62,7 +62,7 @@
 
 def summed_spectra(mic_rows, geom_blocks, source_blocks):
     local_terms = panel_spectra(mic_rows, geom_blocks, source_blocks)
-    return lax.psum(local_terms, "pan")
+    return jnp.sum(lax.all_gather(local_terms, "pan"), axis=0)
 
 
 def cross_terms(own_rows, columns):

time: 1560 us -> 1080 us (0.69)
  waiting for transfers between devices: 1270 us -> 756 us
  local copies, waits for them, and re-layouts: 35.8 us -> 53.4 us
    psum x1 -> x0, waiting for transfers between devices: 1200 us -> none  [summed_spectra(): return lax.psum(local_terms, 'pan')]
    all_gather x0 -> x1, waiting for transfers between devices: none -> 647 us  [summed_spectra(): return jnp.sum(lax.all_gather(local_terms, 'pan'), axis=0)]
    reduce_scatter x1, waiting for transfers between devices: 61.8 us -> 109 us  [shards(): lax.psum_scatter(partial_csm, 'seg', scatter_dimension=2, tiled=True)]
    unnamed x8 -> x9, local copies, waits for them, and re-layouts: 3.77 us -> 21.3 us
where the time goes in v1:
time: 1080 us; the launch traced here: 1070 us
  waiting for transfers between devices  756 us (70%)
  other arithmetic  208 us (19%)
  local copies, waits for them, and re-layouts  53.4 us (5%)
  matrix products  42.3 us (4%)
  between operations  13.5 us (1%)
    all_gather x1, waiting for transfers between devices, summed_spectra(): return jnp.sum(lax.all_gather(local_terms, 'pan'), axis=0)  647 us
    another operation x16, other arithmetic  196 us
    reduce_scatter x1, waiting for transfers between devices, shards(): lax.psum_scatter(partial_csm, 'seg', scatter_dimension=2, tiled=True)  109 us
    dot_general x16, matrix products, step(): jnp.dot(kernel_block(mics, geometry), weights, preferred_element_type=jnp...  41.1 us
  transfers between devices with their start and end apart: 2, of which 2 were waited for; matrix products, arithmetic and copies ran while one was open for 0% of the time, Pallas kernels for 0%

profile of v1, /device:TPU:1, one launch (start us, length us, event | category | flops | bytes accessed | tf_op | source)
XLA Modules:
  0.0 1074.4 jit_solution(11307290253005227977)
XLA Ops:
  9.0 2.8 gather_fusion
  14.1 267.6 %while.13 = (s32[]{:T(128)}, f32[1024,32]{0,1:T(8,128)S(1)}, f32[3,1024]{1,0:T(4,128)S(1)}, f32[16,6,512]{2,1,0:T(8,128)}, bf16[16,2,2,16,512]{4,3,2,1,0:T(8,128...) while((s32[]{:T(128)}, f32[1024,32]{0,1:T(8,128)S(1)}, ...), condition=%wide.region_1.2_spmd.clone, body=%wide.region_0.1_spmd.clone.sunk | while | flops 170999808 | bytes 9150687 | solution.py:59
  15.1 12.3 %subtract_convert_fusion.2 = (bf16[1024,512]{1,0:T(8,128)(2,1)S(1)}, bf16[1024,512]{1,0:T(8,128)(2,1)S(1)}, bf16[1024,512]{1,0:T(8,128)(2,1)S(1)}, bf16[1024,512]{1,0:T(8,128)(2,1)}) fusion(f32[512]{0:T(512)S(1)} %bitcast.81, f32[512]{0:T(512)S(1)} %bitcast.79, f32[1024]{0:T(1024)S(1)} %bitcast.74, f32[512]{0:T(512)S(1)} %bitcast.77, ...), kind=kLoop, calls=%fused_computation.28.clone.1 | loop fusion | flops 18874368 | bytes 4218880 | tf_op jit(solution)/shard_map/convert.2
  31.8 12.3 %subtract_convert_fusion.2 = (bf16[1024,512]{1,0:T(8,128)(2,1)S(1)}, bf16[1024,512]{1,0:T(8,128)(2,1)S(1)}, bf16[1024,512]{1,0:T(8,128)(2,1)S(1)}, bf16[1024,512]{1,0:T(8,128)(2,1)}) fusion(f32[512]{0:T(512)S(1)} %bitcast.81, f32[512]{0:T(512)S(1)} %bitcast.79, f32[1024]{0:T(1024)S(1)} %bitcast.74, f32[512]{0:T(512)S(1)} %bitcast.77, ...), kind=kLoop, calls=%fused_computation.28.clone.1 | loop fusion | flops 18874368 | bytes 4218880 | tf_op jit(solution)/shard_map/convert.2
  48.5 12.3 %subtract_convert_fusion.2 = (bf16[1024,512]{1,0:T(8,128)(2,1)S(1)}, bf16[1024,512]{1,0:T(8,128)(2,1)S(1)}, bf16[1024,512]{1,0:T(8,128)(2,1)S(1)}, bf16[1024,512]{1,0:T(8,128)(2,1)}) fusion(f32[512]{0:T(512)S(1)} %bitcast.81, f32[512]{0:T(512)S(1)} %bitcast.79, f32[1024]{0:T(1024)S(1)} %bitcast.74, f32[512]{0:T(512)S(1)} %bitcast.77, ...), kind=kLoop, calls=%fused_computation.28.clone.1 | loop fusion | flops 18874368 | bytes 4218880 | tf_op jit(solution)/shard_map/convert.2
  65.3 12.3 %subtract_convert_fusion.2 = (bf16[1024,512]{1,0:T(8,128)(2,1)S(1)}, bf16[1024,512]{1,0:T(8,128)(2,1)S(1)}, bf16[1024,512]{1,0:T(8,128)(2,1)S(1)}, bf16[1024,512]{1,0:T(8,128)(2,1)}) fusion(f32[512]{0:T(512)S(1)} %bitcast.81, f32[512]{0:T(512)S(1)} %bitcast.79, f32[1024]{0:T(1024)S(1)} %bitcast.74, f32[512]{0:T(512)S(1)} %bitcast.77, ...), kind=kLoop, calls=%fused_computation.28.clone.1 | loop fusion | flops 18874368 | bytes 4218880 | tf_op jit(solution)/shard_map/convert.2
  82.0 12.3 %subtract_convert_fusion.2 = (bf16[1024,512]{1,0:T(8,128)(2,1)S(1)}, bf16[1024,512]{1,0:T(8,128)(2,1)S(1)}, bf16[1024,512]{1,0:T(8,128)(2,1)S(1)}, bf16[1024,512]{1,0:T(8,128)(2,1)}) fusion(f32[512]{0:T(512)S(1)} %bitcast.81, f32[512]{0:T(512)S(1)} %bitcast.79, f32[1024]{0:T(1024)S(1)} %bitcast.74, f32[512]{0:T(512)S(1)} %bitcast.77, ...), kind=kLoop, calls=%fused_computation.28.clone.1 | loop fusion | flops 18874368 | bytes 4218880 | tf_op jit(solution)/shard_map/convert.2
  95.2 2.6 fusion.66
  98.8 12.3 %subtract_convert_fusion.2 = (bf16[1024,512]{1,0:T(8,128)(2,1)S(1)}, bf16[1024,512]{1,0:T(8,128)(2,1)S(1)}, bf16[1024,512]{1,0:T(8,128)(2,1)S(1)}, bf16[1024,512]{1,0:T(8,128)(2,1)}) fusion(f32[512]{0:T(512)S(1)} %bitcast.81, f32[512]{0:T(512)S(1)} %bitcast.79, f32[1024]{0:T(1024)S(1)} %bitcast.74, f32[512]{0:T(512)S(1)} %bitcast.77, ...), kind=kLoop, calls=%fused_computation.28.clone.1 | loop fusion | flops 18874368 | bytes 4218880 | tf_op jit(solution)/shard_map/convert.2
  111.9 2.6 fusion.66
  115.5 12.3 %subtract_convert_fusion.2 = (bf16[1024,512]{1,0:T(8,128)(2,1)S(1)}, bf16[1024,512]{1,0:T(8,128)(2,1)S(1)}, bf16[1024,512]{1,0:T(8,128)(2,1)S(1)}, bf16[1024,512]{1,0:T(8,128)(2,1)}) fusion(f32[512]{0:T(512)S(1)} %bitcast.81, f32[512]{0:T(512)S(1)} %bitcast.79, f32[1024]{0:T(1024)S(1)} %bitcast.74, f32[512]{0:T(512)S(1)} %bitcast.77, ...), kind=kLoop, calls=%fused_computation.28.clone.1 | loop fusion | flops 18874368 | bytes 4218880 | tf_op jit(solution)/shard_map/convert.2
  132.2 12.3 %subtract_convert_fusion.2 = (bf16[1024,512]{1,0:T(8,128)(2,1)S(1)}, bf16[1024,512]{1,0:T(8,128)(2,1)S(1)}, bf16[1024,512]{1,0:T(8,128)(2,1)S(1)}, bf16[1024,512]{1,0:T(8,128)(2,1)}) fusion(f32[512]{0:T(512)S(1)} %bitcast.81, f32[512]{0:T(512)S(1)} %bitcast.79, f32[1024]{0:T(1024)S(1)} %bitcast.74, f32[512]{0:T(512)S(1)} %bitcast.77, ...), kind=kLoop, calls=%fused_computation.28.clone.1 | loop fusion | flops 18874368 | bytes 4218880 | tf_op jit(solution)/shard_map/convert.2
  148.9 12.3 %subtract_convert_fusion.2 = (bf16[1024,512]{1,0:T(8,128)(2,1)S(1)}, bf16[1024,512]{1,0:T(8,128)(2,1)S(1)}, bf16[1024,512]{1,0:T(8,128)(2,1)S(1)}, bf16[1024,512]{1,0:T(8,128)(2,1)}) fusion(f32[512]{0:T(512)S(1)} %bitcast.81, f32[512]{0:T(512)S(1)} %bitcast.79, f32[1024]{0:T(1024)S(1)} %bitcast.74, f32[512]{0:T(512)S(1)} %bitcast.77, ...), kind=kLoop, calls=%fused_computation.28.clone.1 | loop fusion | flops 18874368 | bytes 4218880 | tf_op jit(solution)/shard_map/convert.2
  165.7 12.3 %subtract_convert_fusion.2 = (bf16[1024,512]{1,0:T(8,128)(2,1)S(1)}, bf16[1024,512]{1,0:T(8,128)(2,1)S(1)}, bf16[1024,512]{1,0:T(8,128)(2,1)S(1)}, bf16[1024,512]{1,0:T(8,128)(2,1)}) fusion(f32[512]{0:T(512)S(1)} %bitcast.81, f32[512]{0:T(512)S(1)} %bitcast.79, f32[1024]{0:T(1024)S(1)} %bitcast.74, f32[512]{0:T(512)S(1)} %bitcast.77, ...), kind=kLoop, calls=%fused_computation.28.clone.1 | loop fusion | flops 18874368 | bytes 4218880 | tf_op jit(solution)/shard_map/convert.2
  182.4 12.3 %subtract_convert_fusion.2 = (bf16[1024,512]{1,0:T(8,128)(2,1)S(1)}, bf16[1024,512]{1,0:T(8,128)(2,1)S(1)}, bf16[1024,512]{1,0:T(8,128)(2,1)S(1)}, bf16[1024,512]{1,0:T(8,128)(2,1)}) fusion(f32[512]{0:T(512)S(1)} %bitcast.81, f32[512]{0:T(512)S(1)} %bitcast.79, f32[1024]{0:T(1024)S(1)} %bitcast.74, f32[512]{0:T(512)S(1)} %bitcast.77, ...), kind=kLoop, calls=%fused_computation.28.clone.1 | loop fusion | flops 18874368 | bytes 4218880 | tf_op jit(solution)/shard_map/convert.2
  199.1 12.3 %subtract_convert_fusion.2 = (bf16[1024,512]{1,0:T(8,128)(2,1)S(1)}, bf16[1024,512]{1,0:T(8,128)(2,1)S(1)}, bf16[1024,512]{1,0:T(8,128)(2,1)S(1)}, bf16[1024,512]{1,0:T(8,128)(2,1)}) fusion(f32[512]{0:T(512)S(1)} %bitcast.81, f32[512]{0:T(512)S(1)} %bitcast.79, f32[1024]{0:T(1024)S(1)} %bitcast.74, f32[512]{0:T(512)S(1)} %bitcast.77, ...), kind=kLoop, calls=%fused_computation.28.clone.1 | loop fusion | flops 18874368 | bytes 4218880 | tf_op jit(solution)/shard_map/convert.2
  215.8 12.3 %subtract_convert_fusion.2 = (bf16[1024,512]{1,0:T(8,128)(2,1)S(1)}, bf16[1024,512]{1,0:T(8,128)(2,1)S(1)}, bf16[1024,512]{1,0:T(8,128)(2,1)S(1)}, bf16[1024,512]{1,0:T(8,128)(2,1)}) fusion(f32[512]{0:T(512)S(1)} %bitcast.81, f32[512]{0:T(512)S(1)} %bitcast.79, f32[1024]{0:T(1024)S(1)} %bitcast.74, f32[512]{0:T(512)S(1)} %bitcast.77, ...), kind=kLoop, calls=%fused_computation.28.clone.1 | loop fusion | flops 18874368 | bytes 4218880 | tf_op jit(solution)/shard_map/convert.2
  232.6 12.3 %subtract_convert_fusion.2 = (bf16[1024,512]{1,0:T(8,128)(2,1)S(1)}, bf16[1024,512]{1,0:T(8,128)(2,1)S(1)}, bf16[1024,512]{1,0:T(8,128)(2,1)S(1)}, bf16[1024,512]{1,0:T(8,128)(2,1)}) fusion(f32[512]{0:T(512)S(1)} %bitcast.81, f32[512]{0:T(512)S(1)} %bitcast.79, f32[1024]{0:T(1024)S(1)} %bitcast.74, f32[512]{0:T(512)S(1)} %bitcast.77, ...), kind=kLoop, calls=%fused_computation.28.clone.1 | loop fusion | flops 18874368 | bytes 4218880 | tf_op jit(solution)/shard_map/convert.2
  249.3 12.3 %subtract_convert_fusion.2 = (bf16[1024,512]{1,0:T(8,128)(2,1)S(1)}, bf16[1024,512]{1,0:T(8,128)(2,1)S(1)}, bf16[1024,512]{1,0:T(8,128)(2,1)S(1)}, bf16[1024,512]{1,0:T(8,128)(2,1)}) fusion(f32[512]{0:T(512)S(1)} %bitcast.81, f32[512]{0:T(512)S(1)} %bitcast.79, f32[1024]{0:T(1024)S(1)} %bitcast.74, f32[512]{0:T(512)S(1)} %bitcast.77, ...), kind=kLoop, calls=%fused_computation.28.clone.1 | loop fusion | flops 18874368 | bytes 4218880 | tf_op jit(solution)/shard_map/convert.2
  266.0 12.3 %subtract_convert_fusion.2 = (bf16[1024,512]{1,0:T(8,128)(2,1)S(1)}, bf16[1024,512]{1,0:T(8,128)(2,1)S(1)}, bf16[1024,512]{1,0:T(8,128)(2,1)S(1)}, bf16[1024,512]{1,0:T(8,128)(2,1)}) fusion(f32[512]{0:T(512)S(1)} %bitcast.81, f32[512]{0:T(512)S(1)} %bitcast.79, f32[1024]{0:T(1024)S(1)} %bitcast.74, f32[512]{0:T(512)S(1)} %bitcast.77, ...), kind=kLoop, calls=%fused_computation.28.clone.1 | loop fusion | flops 18874368 | bytes 4218880 | tf_op jit(solution)/shard_map/convert.2
  282.5 647.1 %all-gather.3.cloned.1.call-done = f32[131072,32]{0,1:T(8,128)} async-done(((f32[1024,32]{0,1:T(8,128)}), f32[131072,32]{0,1:T(8,128)}) %all-gather.3.cloned.1.call-update) | async-done | bytes 16777232 | tf_op jit(solution)/shard_map/all_gather | solution.py:65
  929.6 17.7 %copy.14 = f32[4,8,128,1024]{3,2,1,0:T(8,128)} copy(f32[4,8,128,1024]{3,1,2,0:T(8,128)} %bitcast.70) | data formatting | bytes 33554432
  947.2 8.1 bitcast_reduce_fusion
  957.2 109.1 %reduce-scatter.2.cloned.1.call-done = f32[2,8,256]{2,1,0:T(8,128)} async-done(((f32[2,8,1024]{2,1,0:T(8,128)}), f32[2,8,256]{2,1,0:T(8,128)}) %reduce-scatter.2.cloned.1.call-update) | async-done | bytes 16400 | tf_op jit(solution)/shard_map/reduce_scatter | solution.py:98
  (116 shorter events, 73.9 us)
Async XLA Ops:
  6.5 5.6 copy-start
  6.5 923.0 %all-gather.3.cloned.1.call-start = ((), (), s32[]{:S(2)}) async-start(), calls=%async_computation.2 | async-start | bytes 16908288 | tf_op jit(solution)/shard_map/all_gather | solution.py:65
  281.7 0.7 copy-start.1
  282.4 783.8 %reduce-scatter.2.cloned.1.call-start = ((), (), s32[]{:S(2)}) async-start(), calls=%async_computation.1 | async-start | bytes 81920 | tf_op jit(solution)/shard_map/reduce_scatter | solution.py:98
Sparse Core Ops, SparseCore 0:
  282.5 646.9 all-gather.2
  957.3 108.9 reduce-scatter.1
